TPU v7x, 1024 devices: a whole 4x4x32 slice. The times are simulated.
1024 devices in a mesh: dp: 64 (over z, y_lo), expert: 8 (over x, y_hi), tensor: 2 (over core).
Axes of the slice: x: 4, y: 4 (y_hi: 2, y_lo: 2; y = y_hi * 2 + y_lo), z: 32, core: 2. Of those that a mesh axis runs over, the one named last changes fastest.
Arguments:
- tokens: bfloat16 [65536, 4096], P(('dp', 'expert')), may hold values from -6 to 6
- grads_out: bfloat16 [65536, 4096], P(('dp', 'expert')), may hold values from -6 to 6
- expert_ids: int32 [65536, 1], P(('dp', 'expert')), may hold values from 0 to 7; in each aligned block of 128 rows (0 to 127, 128 to 255, ...) at most 20 rows name the same one
- gate_weights: float32 [65536, 1], P(('dp', 'expert')), may hold values from 0.1 to 0.9
- layout_map: int32 [65536], P(('dp', 'expert')), may hold values from 0 to 127, as said below
- gate_w: bfloat16 [8, 4096, 768], P('expert', None, 'tensor'), may hold values from -0.09375 to 0.09375
- up_w: bfloat16 [8, 4096, 768], P('expert', None, 'tensor'), may hold values from -0.09375 to 0.09375
- down_w: bfloat16 [8, 768, 4096], P('expert', 'tensor'), may hold values from -0.21875 to 0.21875
Outputs:
- layer_out: bfloat16 [65536, 4096], P(('dp', 'expert', 'tensor'))
- input_grad: bfloat16 [65536, 4096], P(('dp', 'expert', 'tensor'))
Inputs may be any that keep to these rules, and one draw needn't show every extreme that they name: `expert_ids`: each row names one expert. Within each aligned block of 128 rows (the tokens of one index of dp and expert) no expert is named by more than 20 rows, a bound that some block reaches. `layout_map`: within each aligned block of 128 tokens the values are a permutation of 0 to 127.
All inputs are finite; a program needn't handle non-finite values.
Results may differ from a plain program's by a relative error of at most 0.0065.
Values may be sent and summed in bfloat16 or wider, within the bound.
A program may use at most 64 MiB of HBM per device.

v0:
```python
import jax
import jax.numpy as jnp
from jax import lax
from jax.sharding import PartitionSpec as P


def shards(tokens, grads_out, expert_ids, gate_weights, layout_map, gate_w, up_w, down_w):
    tok_count, model_width = tokens.shape
    top_count = expert_ids.shape[1]
    expert_count = lax.axis_size("expert")
    slot_cap = tok_count * top_count * 5 // (4 * expert_count)
    pair_count = tok_count * top_count
    slot_total = expert_count * slot_cap
    flat_ids = expert_ids.reshape(pair_count)
    onehot = (flat_ids[:, None] == jnp.arange(expert_count, dtype=jnp.int32)[None, :]).astype(
        jnp.int32
    )
    before = jnp.cumsum(onehot, axis=0) - onehot
    slot_rank = jnp.sum(before * onehot, axis=1)
    slot_index = flat_ids * slot_cap + slot_rank
    slot_match = (slot_index[None, :] == jnp.arange(slot_total, dtype=jnp.int32)[:, None]).astype(
        jnp.int32
    )
    pair_index = jnp.sum(slot_match * jnp.arange(pair_count, dtype=jnp.int32)[None, :], axis=1)
    is_filled = jnp.sum(slot_match, axis=1)
    source_token = pair_index // top_count
    slot_gate = gate_weights.reshape(pair_count)[pair_index] * is_filled.astype(jnp.float32)
    expert_in = (tokens[source_token] * is_filled.astype(jnp.bfloat16)[:, None]).reshape(
        expert_count, slot_cap, model_width
    )
    grad_in = (grads_out[source_token].astype(jnp.float32) * slot_gate[:, None]).astype(
        jnp.bfloat16
    )
    grad_in = grad_in.reshape(expert_count, slot_cap, model_width)
    gate_local = gate_w[0]
    up_local = up_w[0]
    down_local = down_w[0]
    recv_in, recv_grad = (
        lax.all_to_all(expert_in, "expert", split_axis=0, concat_axis=0, tiled=True),
        lax.all_to_all(grad_in, "expert", split_axis=0, concat_axis=0, tiled=True),
    )
    rows_in = recv_in.reshape(slot_total, model_width)
    rows_back = recv_grad.reshape(slot_total, model_width)
    pre_gate = jnp.dot(rows_in, gate_local, preferred_element_type=jnp.float32)
    pre_up = jnp.dot(rows_in, up_local, preferred_element_type=jnp.float32)
    sigma = jax.nn.sigmoid(pre_gate)
    active = pre_gate * sigma
    hidden = (active * pre_up).astype(jnp.bfloat16)
    part_out = jnp.dot(hidden, down_local, preferred_element_type=jnp.float32).astype(jnp.bfloat16)
    grad_hidden = lax.dot_general(
        rows_back, down_local, (((1,), (1,)), ((), ())), preferred_element_type=jnp.float32
    )
    grad_gate = (grad_hidden * pre_up * sigma * (1.0 + pre_gate * (1.0 - sigma))).astype(
        jnp.bfloat16
    )
    grad_up = (grad_hidden * active).astype(jnp.bfloat16)
    part_grad = (
        lax.dot_general(
            grad_gate, gate_local, (((1,), (1,)), ((), ())), preferred_element_type=jnp.float32
        )
        + lax.dot_general(
            grad_up, up_local, (((1,), (1,)), ((), ())), preferred_element_type=jnp.float32
        )
    ).astype(jnp.bfloat16)
    part_out = part_out.reshape(expert_count, slot_cap, model_width)
    part_grad = part_grad.reshape(expert_count, slot_cap, model_width)
    inverse = (
        jnp.zeros((tok_count,), jnp.int32)
        .at[layout_map]
        .set(jnp.arange(tok_count, dtype=jnp.int32))
    )
    back_out, back_grad = (
        lax.all_to_all(part_out, "expert", split_axis=0, concat_axis=0, tiled=True),
        lax.all_to_all(part_grad, "expert", split_axis=0, concat_axis=0, tiled=True),
    )
    rows_out = back_out.reshape(slot_total, model_width)[slot_index].reshape(
        tok_count, top_count, model_width
    )
    rows_grad = back_grad.reshape(slot_total, model_width)[slot_index].reshape(
        tok_count, top_count, model_width
    )
    placed_out = rows_out[inverse].astype(jnp.float32)
    placed_grad = rows_grad[inverse].astype(jnp.float32)
    summed_out, summed_grad = (
        lax.psum_scatter(
            placed_out.astype(jnp.bfloat16), "tensor", scatter_dimension=0, tiled=True
        ).astype(jnp.float32),
        lax.psum_scatter(
            placed_grad.astype(jnp.bfloat16), "tensor", scatter_dimension=0, tiled=True
        ).astype(jnp.float32),
    )
    half_rows = summed_out.shape[0]
    slot_out = lax.optimization_barrier(summed_out.astype(jnp.bfloat16)).astype(jnp.float32)
    slot_grad = lax.optimization_barrier(summed_grad.astype(jnp.bfloat16)).astype(jnp.float32)
    gates_placed = gate_weights[inverse]
    gates_here = lax.dynamic_slice_in_dim(
        gates_placed, lax.axis_index("tensor") * half_rows, half_rows, 0
    )
    layer_out = jnp.sum(slot_out * gates_here[:, :, None], axis=1).astype(jnp.bfloat16)
    input_grad = jnp.sum(slot_grad, axis=1).astype(jnp.bfloat16)
    return (layer_out, input_grad)


def solution(mesh):
    in_specs = (
        P(("dp", "expert"), None),
        P(("dp", "expert"), None),
        P(("dp", "expert"), None),
        P(("dp", "expert"), None),
        P(("dp", "expert")),
        P("expert", None, "tensor"),
        P("expert", None, "tensor"),
        P("expert", "tensor", None),
    )
    out_specs = (P(("dp", "expert", "tensor"), None), P(("dp", "expert", "tensor"), None))
    return jax.shard_map(shards, mesh=mesh, in_specs=in_specs, out_specs=out_specs, check_vma=False)
```

profile of v0, /device:TPU:1, one launch (start us, length us, event | category | flops | bytes accessed | tf_op | source)
XLA Modules:
  0.0 206.0 jit_solution(2219598899220136266)
XLA Ops:
  7.2 0.0 copy-start
  7.2 0.9 fusion.14
  8.1 0.2 reduce_window_sum.11
  8.2 0.8 select_reduce_fusion.1
  9.1 0.7 multiply_add_fusion
  9.7 0.2 convert_reduce_fusion
  9.9 5.1 %gather_fusion = bf16[160,4096]{1,0:T(8,128)(2,1)} fusion(bf16[128,4096]{1,0:T(8,128)(2,1)} %param.8, s32[1024]{0:T(1024)S(1)} %pad_clamp_fusion.2), kind=kCustom, calls=%fused_computation | custom fusion | bytes 2622080 | tf_op jit(solution)/shard_map/gather | solution.py:28
  15.0 2.4 %gather.27 = bf16[8,20,4096]{2,1,0:T(8,128)(2,1)} reshape(bf16[160,4096]{1,0:T(8,128)(2,1)} %gather_fusion) | data formatting | bytes 2621440 | tf_op jit(solution)/shard_map/gather | solution.py:28
  17.4 0.1 convert_element_type.75
  17.4 2.7 %broadcast_multiply_fusion = bf16[8,20,4096]{2,1,0:T(8,128)(2,1)} fusion(bf16[8,20,4096]{2,1,0:T(8,128)(2,1)} %gather.27, bf16[8,20]{1,0:T(8,128)(2,1)S(1)} %convert_element_type.75), kind=kLoop, calls=%fused_computation.24 | loop fusion | flops 655360 | bytes 2621760 | tf_op jit(solution)/shard_map/mul | solution.py:28
  20.2 0.0 copy-start.1
  20.2 7.6 %all-to-all-start = ((bf16[8,20,4096]{2,1,0:T(8,128)(2,1)}), bf16[8,20,4096]{2,1,0:T(8,128)(2,1)}, u32[]{:S(2)}, u32[]{:S(2)}) async-start(bf16[8,20,4096]{2,1,0:T(8,128)(2,1)} %broadcast_multiply_fusion), calls=%async_computation | async-start | bytes 3145728 | tf_op jit(solution)/shard_map/all_to_all | solution.py:39
  27.8 0.0 copy-done.1
  27.8 1.6 gather_fusion.5
  29.3 0.1 mul.104
  29.4 5.1 %gather_fusion.4 = bf16[160,4096]{1,0:T(8,128)(2,1)} fusion(bf16[128,4096]{1,0:T(8,128)(2,1)} %param.9, s32[1024]{0:T(1024)S(1)} %pad_clamp_fusion.2), kind=kCustom, calls=%fused_computation.4 | custom fusion | bytes 2622080 | tf_op jit(solution)/shard_map/gather | solution.py:31
  34.5 2.9 %reshape.109 = f32[8,20,4096]{2,1,0:T(8,128)} reshape(bf16[160,4096]{1,0:T(8,128)(2,1)} %gather_fusion.4) | data formatting | bytes 3932160 | tf_op jit(solution)/shard_map/convert_element_type | solution.py:31
  37.4 3.4 %multiply_convert_fusion = bf16[8,20,4096]{2,1,0:T(8,128)(2,1)} fusion(f32[8,20,4096]{2,1,0:T(8,128)} %reshape.109, f32[8,20]{1,0:T(8,128)S(1)} %mul.104), kind=kLoop, calls=%fused_computation.22 | loop fusion | flops 1310720 | bytes 3932800 | tf_op jit(solution)/shard_map/convert_element_type | solution.py:31
  40.7 1.1 all-to-all-done
  41.8 5.6 %all-to-all-start.2 = ((bf16[8,20,4096]{2,1,0:T(8,128)(2,1)}), bf16[8,20,4096]{2,1,0:T(8,128)(2,1)}, u32[]{:S(2)}, u32[]{:S(2)}) async-start(bf16[8,20,4096]{2,1,0:T(8,128)(2,1)} %multiply_convert_fusion), calls=%async_computation.3 | async-start | bytes 3145728 | tf_op jit(solution)/shard_map/all_to_all | solution.py:40
  47.4 2.4 %reshape.100 = bf16[160,4096]{1,0:T(8,128)(2,1)} reshape(bf16[8,20,4096]{2,1,0:T(8,128)(2,1)} %all-to-all-done) | data formatting | bytes 2621440 | tf_op jit(solution)/shard_map/reshape | solution.py:42
  49.7 0.0 copy-start.3
  49.7 3.3 %fusion.9 = f32[160,384]{1,0:T(8,128)S(1)} fusion(bf16[160,4096]{1,0:T(8,128)(2,1)} %reshape.100, bf16[1,4096,384]{2,1,0:T(8,128)(2,1)} %param.13), kind=kOutput, calls=%fused_computation.20 | convolution fusion | flops 503316480 | bytes 4702208 | tf_op jit(solution)/shard_map/dot_general | solution.py:44
  53.0 0.0 copy-done.3
  53.0 0.3 copy-done.5
  53.3 0.8 fusion.5
  54.2 0.0 copy-start.6
  54.2 0.7 copy-done.6
  54.9 0.0 copy-done
  54.9 2.0 convolution_convert_fusion
  56.9 2.4 %reshape.101 = bf16[8,20,4096]{2,1,0:T(8,128)(2,1)} reshape(bf16[160,4096]{1,0:T(8,128)(2,1)} %convolution_convert_fusion) | data formatting | bytes 2621440 | tf_op jit(solution)/shard_map/reshape | solution.py:65
  59.3 2.6 %all-to-all-done.2 = bf16[8,20,4096]{2,1,0:T(8,128)(2,1)} async-done(((bf16[8,20,4096]{2,1,0:T(8,128)(2,1)}), bf16[8,20,4096]{2,1,0:T(8,128)(2,1)}, u32[]{:S(2)}, u32[]{:S(2)}) %all-to-all-start.2) | async-done | bytes 1310752 | tf_op jit(solution)/shard_map/all_to_all | solution.py:40
  61.8 4.9 %all-to-all-start.1 = ((bf16[8,20,4096]{2,1,0:T(8,128)(2,1)}), bf16[8,20,4096]{2,1,0:T(8,128)(2,1)}, u32[]{:S(2)}, u32[]{:S(2)}) async-start(bf16[8,20,4096]{2,1,0:T(8,128)(2,1)} %reshape.101), calls=%async_computation.1 | async-start | bytes 3145728 | tf_op jit(solution)/shard_map/all_to_all | solution.py:73
  66.7 0.0 reduce-scatter.3.cloned.1.call-start
  66.8 0.0 copy-done.9
  66.8 1.2 scatter_custom_fusion
  68.0 0.0 copy-done.8
  68.1 2.4 %reshape.105 = bf16[160,4096]{1,0:T(8,128)(2,1)} reshape(bf16[8,20,4096]{2,1,0:T(8,128)(2,1)} %all-to-all-done.2) | data formatting | bytes 2621440 | tf_op jit(solution)/shard_map/reshape | solution.py:43
  70.5 12.3 %all-to-all-done.1 = bf16[8,20,4096]{2,1,0:T(8,128)(2,1)} async-done(((bf16[8,20,4096]{2,1,0:T(8,128)(2,1)}), bf16[8,20,4096]{2,1,0:T(8,128)(2,1)}, u32[]{:S(2)}, u32[]{:S(2)}) %all-to-all-start.1) | async-done | bytes 1310752 | tf_op jit(solution)/shard_map/all_to_all | solution.py:73
  82.7 2.3 %reshape.102 = bf16[160,4096]{1,0:T(8,128)(2,1)} reshape(bf16[8,20,4096]{2,1,0:T(8,128)(2,1)} %all-to-all-done.1) | data formatting | bytes 2621440 | tf_op jit(solution)/shard_map/reshape | solution.py:76
  85.1 4.7 %gather_fusion.1 = bf16[128,4096]{1,0:T(8,128)(2,1)} fusion(bf16[160,4096]{1,0:T(8,128)(2,1)} %reshape.102, s32[1024]{0:T(1024)S(1)} %pad_clamp_fusion.1), kind=kCustom, calls=%fused_computation.1 | custom fusion | bytes 2097664 | tf_op jit(solution)/shard_map/gather | solution.py:76
  89.8 4.6 %gather_fusion.2 = bf16[128,4096]{1,0:T(8,128)(2,1)} fusion(bf16[128,4096]{1,0:T(8,128)(2,1)} %gather_fusion.1, s32[1024]{0:T(1024)S(1)} %pad_clamp_fusion), kind=kCustom, calls=%fused_computation.2 | custom fusion | bytes 2097664 | tf_op jit(solution)/shard_map/gather | solution.py:82
  94.3 0.0 reduce-scatter.3.cloned.1.call-update
  94.3 0.0 reduce-scatter.5.cloned.1.call-start
  94.4 0.0 copy-start.2
  94.4 0.0 copy-start.7
  94.4 2.6 %fusion.1 = f32[160,384]{1,0:T(8,128)S(1)} fusion(bf16[160,4096]{1,0:T(8,128)(2,1)} %reshape.105, bf16[1,384,4096]{2,1,0:T(8,128)(2,1)S(1)} %copy-done), kind=kOutput, calls=%fused_computation.12 | convolution fusion | flops 503316480 | bytes 4702208 | tf_op jit(solution)/shard_map/dot_general | solution.py:50
  97.0 0.0 copy-done.2
  97.0 0.0 copy-done.7
  97.0 0.0 copy-start.4
  97.0 1.2 fusion.7
  98.2 0.7 copy-done.4
  98.9 2.2 %fusion = bf16[160,4096]{1,0:T(8,128)(2,1)} fusion(f32[160,4096]{1,0:T(8,128)S(1)} %fusion.7, bf16[1,4096,384]{2,1,0:T(8,128)(2,1)S(1)} %copy-done.4, f32[160,384]{1,0:T(8,128)S(1)} %fusion.1, f32[160,384]{1,0:T(8,128)S(1)} %fusion.9), kind=kOutput, calls=%fused_computation.10 | convolution fusion | flops 504995840 | bytes 7569408 | tf_op jit(solution)/shard_map/dot_general | solution.py:61
  101.2 2.4 %reshape.106 = bf16[8,20,4096]{2,1,0:T(8,128)(2,1)} reshape(bf16[160,4096]{1,0:T(8,128)(2,1)} %fusion) | data formatting | bytes 2621440 | tf_op jit(solution)/shard_map/reshape | solution.py:66
  103.5 18.9 %all_to_all.20 = bf16[8,20,4096]{2,1,0:T(8,128)(2,1)} all-to-all(bf16[8,20,4096]{2,1,0:T(8,128)(2,1)} %reshape.106), channel_id=1, replica_groups=mesh['dp'=64,'expert'=8,'tensor'=2] {'expert'}, dimensions={0} | all-to-all | bytes 2621440 | tf_op jit(solution)/shard_map/all_to_all | solution.py:74
  122.5 2.3 %reshape.107 = bf16[160,4096]{1,0:T(8,128)(2,1)} reshape(bf16[8,20,4096]{2,1,0:T(8,128)(2,1)} %all_to_all.20) | data formatting | bytes 2621440 | tf_op jit(solution)/shard_map/reshape | solution.py:79
  124.8 4.7 %gather_fusion.6 = bf16[128,4096]{1,0:T(8,128)(2,1)} fusion(bf16[160,4096]{1,0:T(8,128)(2,1)} %reshape.107, s32[1024]{0:T(1024)S(1)} %pad_clamp_fusion.1), kind=kCustom, calls=%fused_computation.6 | custom fusion | bytes 2097664 | tf_op jit(solution)/shard_map/gather | solution.py:79
  129.5 4.5 %gather_fusion.7 = bf16[128,4096]{1,0:T(8,128)(2,1)} fusion(bf16[128,4096]{1,0:T(8,128)(2,1)} %gather_fusion.6, s32[1024]{0:T(1024)S(1)} %pad_clamp_fusion), kind=kCustom, calls=%fused_computation.7 | custom fusion | bytes 2097664 | tf_op jit(solution)/shard_map/gather | solution.py:83
  134.0 0.0 reduce-scatter.5.cloned.1.call-update
  134.0 1.2 gather_fusion.3
  135.3 0.1 dynamic-slice
  135.3 16.8 %reduce-scatter.3.cloned.1.call-done = bf16[64,1,4096]{2,0,1:T(8,128)(2,1)} async-done(((bf16[128,1,4096]{2,0,1:T(8,128)(2,1)}), bf16[64,1,4096]{2,0,1:T(8,128)(2,1)}) %reduce-scatter.3.cloned.1.call-update) | async-done | bytes 524304 | tf_op jit(solution)/shard_map/reduce_scatter | solution.py:85
  152.2 2.0 fusion.11
  154.2 45.0 %reduce-scatter.5.cloned.1.call-done = bf16[64,1,4096]{2,0,1:T(8,128)(2,1)} async-done(((bf16[128,1,4096]{2,0,1:T(8,128)(2,1)}), bf16[64,1,4096]{2,0,1:T(8,128)(2,1)}) %reduce-scatter.5.cloned.1.call-update) | async-done | bytes 524304 | tf_op jit(solution)/shard_map/reduce_scatter | solution.py:88
  (13 shorter events, 0.1 us)
Async XLA Ops:
  7.2 47.7 %copy-start = (bf16[1,384,4096]{2,1,0:T(8,128)(2,1)S(1)}, bf16[1,384,4096]{2,1,0:T(8,128)(2,1)}, u32[]{:S(2)}) copy-start(bf16[1,384,4096]{2,1,0:T(8,128)(2,1)} %param.15) | copy-start | bytes 9437188
  20.2 7.6 %copy-start.1 = (f32[128,1]{0,1:T(1,128)S(1)}, f32[128,1]{0,1:T(1,128)}, u32[]{:S(2)}) copy-start(f32[128,1]{0,1:T(1,128)} %param.11) | copy-start | bytes 1540
  20.2 21.7 %all-to-all-start = ((bf16[8,20,4096]{2,1,0:T(8,128)(2,1)}), bf16[8,20,4096]{2,1,0:T(8,128)(2,1)}, u32[]{:S(2)}, u32[]{:S(2)}) async-start(bf16[8,20,4096]{2,1,0:T(8,128)(2,1)} %broadcast_multiply_fusion), calls=%async_computation | async-start | bytes 3145728 | tf_op jit(solution)/shard_map/all_to_all | solution.py:39
  41.8 20.0 %all-to-all-start.2 = ((bf16[8,20,4096]{2,1,0:T(8,128)(2,1)}), bf16[8,20,4096]{2,1,0:T(8,128)(2,1)}, u32[]{:S(2)}, u32[]{:S(2)}) async-start(bf16[8,20,4096]{2,1,0:T(8,128)(2,1)} %multiply_convert_fusion), calls=%async_computation.3 | async-start | bytes 3145728 | tf_op jit(solution)/shard_map/all_to_all | solution.py:40
  49.7 3.3 %copy-start.3 = (bf16[1,4096,384]{2,1,0:T(8,128)(2,1)S(1)}, bf16[1,4096,384]{2,1,0:T(8,128)(2,1)}, u32[]{:S(2)}) copy-start(bf16[1,4096,384]{2,1,0:T(8,128)(2,1)} %param.14) | copy-start | bytes 9437188
  49.7 3.6 %copy-start.5 = (bf16[160,4096]{1,0:T(8,128)(2,1)S(1)}, bf16[160,4096]{1,0:T(8,128)(2,1)}, u32[]{:S(2)}) copy-start(bf16[160,4096]{1,0:T(8,128)(2,1)} %reshape.100) | copy-start | bytes 3932164
  54.2 0.7 copy-start.6
  59.3 7.5 %copy-start.9 = (s32[128]{0:T(128)S(1)}, s32[128]{0:T(128)}, u32[]{:S(2)}) copy-start(s32[128]{0:T(128)} %param.12) | copy-start | bytes 1540
  59.3 8.7 %copy-start.8 = (s32[128,1]{0,1:T(1,128)S(1)}, s32[128,1]{0,1:T(1,128)}, u32[]{:S(2)}) copy-start(s32[128,1]{0,1:T(1,128)} %param.10) | copy-start | bytes 1540
  61.8 20.9 %all-to-all-start.1 = ((bf16[8,20,4096]{2,1,0:T(8,128)(2,1)}), bf16[8,20,4096]{2,1,0:T(8,128)(2,1)}, u32[]{:S(2)}, u32[]{:S(2)}) async-start(bf16[8,20,4096]{2,1,0:T(8,128)(2,1)} %reshape.101), calls=%async_computation.1 | async-start | bytes 3145728 | tf_op jit(solution)/shard_map/all_to_all | solution.py:73
  66.7 85.4 %reduce-scatter.3.cloned.1.call-start = ((), (), s32[]{:S(2)}) async-start(), calls=%async_computation.6 | async-start | bytes 1572864 | tf_op jit(solution)/shard_map/reduce_scatter | solution.py:85
  94.3 104.8 %reduce-scatter.5.cloned.1.call-start = ((), (), s32[]{:S(2)}) async-start(), calls=%async_computation.7 | async-start | bytes 1572864 | tf_op jit(solution)/shard_map/reduce_scatter | solution.py:88
  94.4 2.6 %copy-start.2 = (bf16[1,4096,384]{2,1,0:T(8,128)(2,1)S(1)}, bf16[1,4096,384]{2,1,0:T(8,128)(2,1)}, u32[]{:S(2)}) copy-start(bf16[1,4096,384]{2,1,0:T(8,128)(2,1)} %param.13) | copy-start | bytes 9437188
  94.4 2.6 %copy-start.7 = (f32[160,384]{1,0:T(8,128)S(1)}, f32[160,384]{1,0:T(8,128)}, u32[]{:S(2)}) copy-start(f32[160,384]{1,0:T(8,128)} %copy-done.6) | copy-start | bytes 737284
  97.0 1.9 copy-start.4
Sparse Core Ops, SparseCore 0:
  94.5 57.6 reduce-scatter.2
  156.1 42.9 reduce-scatter.4
where the time goes:
time: 207 us; the launch traced here: 206 us
  waiting for transfers between devices  77.8 us (38%)
  local copies, waits for them, and re-layouts  53.9 us (26%)
  blocking collectives  18.9 us (9%)
  starting transfers between devices  18.1 us (9%)
  between operations  14.3 us (7%)
  matrix products  12.1 us (6%)
  other arithmetic  10.8 us (5%)
    reduce_scatter x1, waiting for transfers between devices, shards(): lax.psum_scatter(placed_grad.astype(jnp.bfloat16), 'tensor', scatter_dime...  45 us
    all_to_all x1, blocking collectives, shards(): lax.all_to_all(part_grad, 'expert', split_axis=0, concat_axis=0, tiled=True)  18.9 us
    reduce_scatter x1, waiting for transfers between devices, shards(): lax.psum_scatter(placed_out.astype(jnp.bfloat16), 'tensor', scatter_dimen...  16.8 us
    all_to_all x1, waiting for transfers between devices, shards(): lax.all_to_all(part_out, 'expert', split_axis=0, concat_axis=0, tiled=True)  12.3 us
    all_to_all x1, starting transfers between devices, shards(): lax.all_to_all(expert_in, 'expert', split_axis=0, concat_axis=0, tiled=True)  7.6 us
    gather x2, local copies, waits for them, and re-layouts, shards(): tokens[source_token] * is_filled.astype(jnp.bfloat16)[:, None]  7.42 us
    all_to_all x1, starting transfers between devices, shards(): lax.all_to_all(grad_in, 'expert', split_axis=0, concat_axis=0, tiled=True)  5.56 us
    gather x1, local copies, waits for them, and re-layouts, shards(): grads_out[source_token].astype(jnp.float32) * slot_gate[:, None]  5.08 us
  transfers between devices with their start and end apart: 5, of which 5 were waited for; matrix products, arithmetic and copies ran while one was open for 25% of the time, Pallas kernels for 0%

commit v1 on v0

v1 whole, which is shorter than its diff:
```python
import functools

import jax
import jax.numpy as jnp
from jax import lax
from jax.experimental import pallas as pl
from jax.experimental.pallas import tpu as pltpu
from jax.sharding import PartitionSpec as P

MESH = pl.DeviceIdType.MESH
BF, F32 = jnp.bfloat16, jnp.float32


def iota(shape, axis):
    return lax.broadcasted_iota(jnp.int32, shape, axis)


def dot(a, b):
    return jnp.dot(a, b, preferred_element_type=F32)


def dot_t(a, b):
    return lax.dot_general(a, b, (((1,), (1,)), ((), ())), preferred_element_type=F32)


def one_hot(mask):
    return jnp.where(mask, 1.0, 0.0).astype(BF)


def kernel(
    experts, cap,
    ids_ref, gates_ref, layout_ref, tokens_ref, grads_ref, wg_hbm, wu_hbm, wd_hbm,
    out_ref, grad_ref,
    rows, send_main, send_left, x_all, left_all, wg, wu, wd,
    pre_gate, pre_up, hidden, grad_gate, grad_up, part_away, part_home, part_recv,
    back_main, back_left, home_main, home_left, pick_main, pick_left, gate_row, away_out,
    in_sem, w_sem, disp_s, disp_r, fwd_s, fwd_r, part_s, part_r, ret_s, ret_r, end_s, end_r,
):
    me, core = lax.axis_index("expert"), lax.axis_index("tensor")
    tok, width = tokens_ref.shape
    half = width // 2
    quarter = half // 4
    peers = experts - 1
    main = 16 * experts
    extra = cap - 16
    half_rows = tok // 2
    partner = {"tensor": 1 - core}
    mine = pl.multiple_of(core * half, 128)
    other = pl.multiple_of((1 - core) * half, 128)

    def peer(k):
        x, y = me // 2, me % 2
        return ((x + k // 2) % (experts // 2)) * 2 + (y + k) % 2

    def source(k):
        x, y = me // 2, me % 2
        return ((x + experts // 2 - k // 2) % (experts // 2)) * 2 + (y + k) % 2

    barrier = pltpu.get_barrier_semaphore()
    for k in range(1, experts):
        pl.semaphore_signal(barrier, inc=1, device_id={"expert": peer(k)}, device_id_type=MESH)
    pl.semaphore_signal(barrier, inc=1, device_id=partner, device_id_type=MESH)

    loads = [
        pltpu.make_async_copy(tokens_ref.at[:, pl.ds(mine, half)], rows.at[0], in_sem.at[0]),
        pltpu.make_async_copy(grads_ref.at[:, pl.ds(mine, half)], rows.at[1], in_sem.at[1]),
    ]
    weights = [
        pltpu.make_async_copy(wg_hbm, wg, w_sem.at[0]),
        pltpu.make_async_copy(wu_hbm, wu, w_sem.at[1]),
        pltpu.make_async_copy(wd_hbm, wd, w_sem.at[2]),
    ]
    for copy in loads + weights:
        copy.start()

    ids = ids_ref[...]
    named = one_hot(iota((experts, tok), 0) == ids)
    earlier = one_hot(iota((tok, tok), 0) < iota((tok, tok), 1))
    rank = jnp.sum(dot(named, earlier) * named.astype(F32), axis=0, keepdims=True)
    base = ids.astype(F32) * 16.0
    row_id = iota((main, tok), 0).astype(F32)
    main_row = jnp.where(rank < 16.0, base + rank, -1.0)
    to_main = one_hot(row_id == main_row)
    to_left = []
    for q in range(4):
        left_row = jnp.where(rank < 16.0, -1.0, base + (rank - 16.0 + extra * q))
        to_left.append(one_hot(row_id == left_row))
    gates = gates_ref[...]
    same = iota((tok, tok), 0) == iota((tok, tok), 1)
    gate_col = jnp.sum(jnp.where(same, gates, 0.0), axis=1, keepdims=True)

    def dispatch(a, k):
        e = peer(k)
        here, there = pl.ds(pl.multiple_of(e * 16, 16), 16), pl.ds(pl.multiple_of(me * 16, 16), 16)
        return (
            pltpu.make_async_remote_copy(
                send_main.at[a, here], x_all.at[a, there, pl.ds(mine, half)],
                disp_s.at[a, k, 0], disp_r.at[a, k, 0], device_id={"expert": e}, device_id_type=MESH),
            pltpu.make_async_remote_copy(
                send_left.at[a, here], left_all.at[a, core, there],
                disp_s.at[a, k, 1], disp_r.at[a, k, 1], device_id={"expert": e}, device_id_type=MESH),
        )

    def forward(a, k):
        at = pl.ds(pl.multiple_of(source(k) * 16, 16), 16)
        return (
            pltpu.make_async_remote_copy(
                x_all.at[a, at, pl.ds(mine, half)], x_all.at[a, at, pl.ds(mine, half)],
                fwd_s.at[a, k, 0], fwd_r.at[a, k, 0], device_id=partner, device_id_type=MESH),
            pltpu.make_async_remote_copy(
                left_all.at[a, core, at], left_all.at[a, core, at],
                fwd_s.at[a, k, 1], fwd_r.at[a, k, 1], device_id=partner, device_id_type=MESH),
        )

    def arrange(a):
        left = jnp.zeros((main, quarter), F32)
        for q in range(4):
            cols = pl.ds(q * quarter, quarter)
            block = rows[a, :, cols]
            if a == 1:
                block = (block.astype(F32) * gate_col).astype(BF)
            send_main[a, :, cols] = dot(to_main, block).astype(BF)
            left = left + dot(to_left[q], block)
        send_left[a] = left.astype(BF)

    def send_all(a):
        for k in range(1, experts):
            for copy in dispatch(a, k):
                copy.start()
        own = pl.ds(pl.multiple_of(me * 16, 16), 16)
        x_all[a, own, pl.ds(mine, half)] = send_main[a, own]
        left_all[a, core, own] = send_left[a, own]

    def forward_all(a):
        for copy in forward(a, 0):
            copy.start()
        for k in range(1, experts):
            for copy in dispatch(a, k):
                copy.wait_recv()
            for copy in forward(a, k):
                copy.start()

    def forward_wait(a):
        for k in range(experts):
            for copy in forward(a, k):
                copy.wait_recv()

    def spread_left(a):
        r, c = iota((experts * extra, main), 0), iota((experts * extra, main), 1)
        for q in range(4):
            pick = one_hot(c == (r // extra) * 16 + q * extra + r % extra)
            for h in range(2):
                x_all[a, main:, pl.ds(h * half + q * quarter, quarter)] = dot(pick, left_all[a, h]).astype(BF)

    loads[0].wait()
    arrange(0)
    pl.semaphore_wait(barrier, peers + 1)
    send_all(0)
    loads[1].wait()
    arrange(1)
    send_all(1)

    place = one_hot(iota((tok, tok), 0) == layout_ref[...])
    pick_main[...] = dot_t(place, to_main).astype(BF)
    for q in range(4):
        pick_left[q] = dot_t(place, to_left[q]).astype(BF)
    gate_row[...] = jnp.sum(jnp.where(iota((tok, tok), 0) == layout_ref[...], gates, 0.0), axis=1, keepdims=True)

    forward_all(0)
    for copy in weights:
        copy.wait()
    forward_wait(0)
    spread_left(0)
    pre_gate[...] = dot(x_all[0], wg[...])
    pre_up[...] = dot(x_all[0], wu[...])
    hidden[...] = (pre_gate[...] * jax.nn.sigmoid(pre_gate[...]) * pre_up[...]).astype(BF)
    forward_all(1)

    def exchange(a):
        return pltpu.make_async_remote_copy(
            part_away.at[a], part_recv.at[a], part_s.at[a], part_r.at[a], device_id=partner, device_id_type=MESH)

    def out_part(start, ref):
        for q in range(4):
            cols = pl.ds(q * quarter, quarter)
            ref[0, :, cols] = dot(hidden[...], wd[:, pl.ds(pl.multiple_of(start + q * quarter, 128), quarter)]).astype(BF)

    def grad_part(start, ref):
        for q in range(4):
            cols = pl.ds(q * quarter, quarter)
            at = pl.ds(pl.multiple_of(start + q * quarter, 128), quarter)
            ref[1, :, cols] = (dot_t(grad_gate[...], wg[at, :]) + dot_t(grad_up[...], wu[at, :])).astype(BF)

    def give_back(a, k):
        g = peer(k)
        here, there = pl.ds(pl.multiple_of(g * 16, 16), 16), pl.ds(pl.multiple_of(me * 16, 16), 16)
        return (
            pltpu.make_async_remote_copy(
                back_main.at[a, here], home_main.at[a, there],
                ret_s.at[a, k, 0], ret_r.at[a, k, 0], device_id={"expert": g}, device_id_type=MESH),
            pltpu.make_async_remote_copy(
                back_left.at[a, here], home_left.at[a, there],
                ret_s.at[a, k, 1], ret_r.at[a, k, 1], device_id={"expert": g}, device_id_type=MESH),
        )

    def return_all(a):
        exchange(a).wait_recv()
        r, c = iota((main, experts * extra), 0), iota((main, experts * extra), 1)
        packed = jnp.zeros((main, quarter), F32)
        for q in range(4):
            cols = pl.ds(q * quarter, quarter)
            total = (part_home[a, :, cols].astype(F32) + part_recv[a, :, cols].astype(F32)).astype(BF)
            back_main[a, :, cols] = total[:main]
            pick = one_hot(r == (c // extra) * 16 + q * extra + c % extra)
            packed = packed + dot(pick, total[main:])
        back_left[a] = packed.astype(BF)
        for k in range(1, experts):
            for copy in give_back(a, k):
                copy.start()
        own = pl.ds(pl.multiple_of(me * 16, 16), 16)
        home_main[a, own] = back_main[a, own]
        home_left[a, own] = back_left[a, own]

    out_part(other, part_away)
    exchange(0).start()
    out_part(mine, part_home)
    forward_wait(1)
    spread_left(1)
    return_all(0)

    grad_hidden = dot_t(x_all[1], wd[...])
    gate_v, up_v = pre_gate[...], pre_up[...]
    sigma = jax.nn.sigmoid(gate_v)
    grad_gate[...] = (grad_hidden * up_v * sigma * (1.0 + gate_v * (1.0 - sigma))).astype(BF)
    grad_up[...] = (grad_hidden * gate_v * sigma).astype(BF)
    grad_part(other, part_away)
    exchange(1).start()
    grad_part(mine, part_home)
    return_all(1)

    def finish_copy(a, ref):
        return pltpu.make_async_remote_copy(
            away_out.at[a], ref.at[:, pl.ds(mine, half)], end_s.at[a], end_r.at[a],
            device_id=partner, device_id_type=MESH)

    keep = pl.ds(pl.multiple_of(core * half_rows, half_rows), half_rows)
    give = pl.ds(pl.multiple_of((1 - core) * half_rows, half_rows), half_rows)

    def finish(a, ref):
        for k in range(1, experts):
            for copy in give_back(a, k):
                copy.wait_recv()

        def placed(at, q):
            cols = pl.ds(q * quarter, quarter)
            value = dot(pick_main[at], home_main[a, :, cols]) + dot(pick_left[q, at], home_left[a])
            if a == 0:
                value = value * gate_row[at]
            return value.astype(BF)

        for q in range(4):
            away_out[a, :, pl.ds(q * quarter, quarter)] = placed(give, q)
        finish_copy(a, ref).start()
        for q in range(4):
            ref[:, pl.ds(pl.multiple_of(mine + q * quarter, 128), quarter)] = placed(keep, q)

    finish(0, out_ref)
    finish(1, grad_ref)

    for a, ref in ((0, out_ref), (1, grad_ref)):
        for k in range(1, experts):
            for copy in dispatch(a, k):
                copy.wait_send()
            for copy in give_back(a, k):
                copy.wait_send()
        for k in range(experts):
            for copy in forward(a, k):
                copy.wait_send()
        exchange(a).wait_send()
        finish_copy(a, ref).wait()


def shards(tokens, grads_out, expert_ids, gate_weights, layout_map, gate_w, up_w, down_w):
    tok, width = tokens.shape
    experts = lax.axis_size("expert")
    hid = gate_w.shape[2]
    cap = tok * 5 // (4 * experts)
    half = width // 2
    quarter = half // 4
    slots, main = experts * cap, experts * 16
    vmem, dma = pltpu.VMEM, pltpu.SemaphoreType.DMA
    in_vmem, anywhere = pl.BlockSpec(memory_space=pltpu.VMEM), pl.BlockSpec(memory_space=pl.ANY)
    out = jax.ShapeDtypeStruct((tok // 2, width), BF)
    return pl.pallas_call(
        functools.partial(kernel, experts, cap),
        out_shape=(out, out),
        in_specs=[in_vmem] * 3 + [anywhere] * 5,
        out_specs=(in_vmem, in_vmem),
        scratch_shapes=[
            vmem((2, tok, half), BF),
            vmem((2, main, half), BF),
            vmem((2, main, quarter), BF),
            vmem((2, slots, width), BF),
            vmem((2, 2, main, quarter), BF),
            vmem((width, hid), BF),
            vmem((width, hid), BF),
            vmem((hid, width), BF),
            vmem((slots, hid), F32),
            vmem((slots, hid), F32),
            vmem((slots, hid), BF),
            vmem((slots, hid), BF),
            vmem((slots, hid), BF),
            vmem((2, slots, half), BF),
            vmem((2, slots, half), BF),
            vmem((2, slots, half), BF),
            vmem((2, main, half), BF),
            vmem((2, main, quarter), BF),
            vmem((2, main, half), BF),
            vmem((2, main, quarter), BF),
            vmem((tok, main), BF),
            vmem((4, tok, main), BF),
            vmem((tok, 1), F32),
            vmem((2, tok // 2, half), BF),
            dma((2,)),
            dma((3,)),
            dma((2, experts, 2)),
            dma((2, experts, 2)),
            dma((2, experts, 2)),
            dma((2, experts, 2)),
            dma((2,)),
            dma((2,)),
            dma((2, experts, 2)),
            dma((2, experts, 2)),
            dma((2,)),
            dma((2,)),
        ],
        compiler_params=pltpu.CompilerParams(collective_id=0, has_side_effects=True, vmem_limit_bytes=60 << 20),
    )(
        expert_ids.reshape(1, tok),
        gate_weights.reshape(1, tok),
        layout_map.reshape(1, tok),
        tokens,
        grads_out,
        gate_w[0],
        up_w[0],
        down_w[0],
    )


def solution(mesh):
    in_specs = (
        P(("dp", "expert"), None),
        P(("dp", "expert"), None),
        P(("dp", "expert"), None),
        P(("dp", "expert"), None),
        P(("dp", "expert")),
        P("expert", None, "tensor"),
        P("expert", None, "tensor"),
        P("expert", "tensor", None),
    )
    out_specs = (P(("dp", "expert", "tensor"), None), P(("dp", "expert", "tensor"), None))
    return jax.shard_map(shards, mesh=mesh, in_specs=in_specs, out_specs=out_specs, check_vma=False)
```

time: 207 us -> 62.8 us (0.30)
  waiting for transfers between devices: 77.8 us -> 0 us
  Pallas kernels: 0 us -> 58.1 us
  local copies, waits for them, and re-layouts: 53.9 us -> 3.74 us
  blocking collectives: 18.9 us -> 0 us
  starting transfers between devices: 18.1 us -> 0 us
  between operations: 14.3 us -> 0.64 us
  matrix products: 12.1 us -> 0 us
  other arithmetic: 10.8 us -> 0 us
    reduce_scatter x2 -> x0, waiting for transfers between devices: 61.8 us -> none  [the longest x1 45 us: shards(): lax.psum_scatter(placed_grad.astype(jnp.bfloat16), 'tensor', scatter_dime...]
    pallas_call x0 -> x1, Pallas kernels: none -> 58.1 us  [shards(): pl.pallas_call(functools.partial(kernel, experts, cap), out_shape=(out, o...]
    gather x9 -> x0, local copies, waits for them, and re-layouts: 33.7 us -> none  [the longest x2 7.42 us: shards(): tokens[source_token] * is_filled.astype(jnp.bfloat16)[:, None]]
    all_to_all x1 -> x0, blocking collectives: 18.9 us -> none  [shards(): lax.all_to_all(part_grad, 'expert', split_axis=0, concat_axis=0, tiled=True)]
    all_to_all x3 -> x0, starting transfers between devices: 18.1 us -> none  [the longest x1 7.6 us: shards(): lax.all_to_all(expert_in, 'expert', split_axis=0, concat_axis=0, tiled=True)]
    all_to_all x3 -> x0, waiting for transfers between devices: 15.9 us -> none  [the longest x1 12.3 us: shards(): lax.all_to_all(part_out, 'expert', split_axis=0, concat_axis=0, tiled=True)]
    reshape x6 -> x0, local copies, waits for them, and re-layouts: 14.2 us -> none  [the longest x1 2.4 us: shards(): rows_back = recv_grad.reshape(slot_total, model_width)]
    dot_general x6 -> x0, matrix products: 12.1 us -> none  [the longest x1 3.28 us: shards(): pre_gate = jnp.dot(rows_in, gate_local, preferred_element_type=jnp.float32)]
  transfers between devices with their start and end apart: 5 -> 0, of which waited for: 5 -> 0; matrix products, arithmetic and copies ran while one was open for 25% -> 0% of each run, Pallas kernels for 0% -> 0%
where the time goes in v1:
time: 62.8 us; the launch traced here: 62.5 us
  Pallas kernels  58.1 us (93%)
  local copies, waits for them, and re-layouts  3.74 us (6%)
  between operations  0.64 us (1%)
    pallas_call x1, Pallas kernels, shards(): pl.pallas_call(functools.partial(kernel, experts, cap), out_shape=(out, o...  58.1 us
    unnamed x2, local copies, waits for them, and re-layouts  3.74 us

profile of v1, /device:TPU:1, one launch (start us, length us, event | category | flops | bytes accessed | tf_op | source)
XLA Modules:
  0.0 62.5 jit_solution(18178358664196989182)
XLA Ops:
  0.6 58.1 %shard_map.95 = (bf16[64,4096]{1,0:T(8,128)(2,1)}, bf16[64,4096]{1,0:T(8,128)(2,1)}) custom-call(s32[1,128]{1,0:T(1,128)} %bitcast.9, f32[1,128]{1,0:T(1,128)} %bitcast.10, s32[1,128]{1,0:T(1,128)} %bitcast.11, bf16[128,4096]{1,0:T(8,128)(2,1)} %tokens_ref.1, bf16[128,4096]{1,0:T(8,128)(2,1)} %grads_ref.1, bf16[4096,384]{1,0:T(8,128)(2,1)} %bitcast.6, ...), custom_call_target="tpu_custom_call" | custom-call | tf_op jit(solution)/shard_map/pallas_call | solution.py:294
  58.8 1.9 %copy.12 = bf16[64,4096]{1,0:T(8,128)(2,1)} copy(bf16[64,4096]{1,0:T(8,128)(2,1)} %get-tuple-element.4) | data formatting | bytes 1048576
  60.6 1.9 %copy.13 = bf16[64,4096]{1,0:T(8,128)(2,1)} copy(bf16[64,4096]{1,0:T(8,128)(2,1)} %get-tuple-element.5) | data formatting | bytes 1048576

commit v2 on v1

--- a/solution.py
+++ b/solution.py
@@ -8,6 +8,7 @@
 from jax.sharding import PartitionSpec as P
 
 MESH = pl.DeviceIdType.MESH
+FAR_FIRST = (5, 3, 7, 4, 1, 2, 6)
 BF, F32 = jnp.bfloat16, jnp.float32
 
 
@@ -29,9 +30,9 @@
 
 def kernel(
     experts, cap,
-    ids_ref, gates_ref, layout_ref, tokens_ref, grads_ref, wg_hbm, wu_hbm, wd_hbm,
+    ids_hbm, gates_hbm, layout_hbm, tokens_ref, grads_ref, wg_hbm, wu_hbm, wd_hbm,
     out_ref, grad_ref,
-    rows, send_main, send_left, x_all, left_all, wg, wu, wd,
+    ids_ref, gates_ref, layout_ref, rows, send_main, send_left, x_all, left_all, wg, wu, wd,
     pre_gate, pre_up, hidden, grad_gate, grad_up, part_away, part_home, part_recv,
     back_main, back_left, home_main, home_left, pick_main, pick_left, gate_row, away_out,
     in_sem, w_sem, disp_s, disp_r, fwd_s, fwd_r, part_s, part_r, ret_s, ret_r, end_s, end_r,
@@ -56,11 +57,11 @@
         x, y = me // 2, me % 2
         return ((x + experts // 2 - k // 2) % (experts // 2)) * 2 + (y + k) % 2
 
-    barrier = pltpu.get_barrier_semaphore()
-    for k in range(1, experts):
-        pl.semaphore_signal(barrier, inc=1, device_id={"expert": peer(k)}, device_id_type=MESH)
-    pl.semaphore_signal(barrier, inc=1, device_id=partner, device_id_type=MESH)
-
+    small = [
+        pltpu.make_async_copy(ids_hbm, ids_ref, in_sem.at[2]),
+        pltpu.make_async_copy(gates_hbm, gates_ref, in_sem.at[3]),
+        pltpu.make_async_copy(layout_hbm, layout_ref, in_sem.at[4]),
+    ]
     loads = [
         pltpu.make_async_copy(tokens_ref.at[:, pl.ds(mine, half)], rows.at[0], in_sem.at[0]),
         pltpu.make_async_copy(grads_ref.at[:, pl.ds(mine, half)], rows.at[1], in_sem.at[1]),
@@ -70,8 +71,14 @@
         pltpu.make_async_copy(wu_hbm, wu, w_sem.at[1]),
         pltpu.make_async_copy(wd_hbm, wd, w_sem.at[2]),
     ]
-    for copy in loads + weights:
+    for copy in [small[0], loads[0], *small[1:], loads[1]]:
         copy.start()
+    barrier = pltpu.get_barrier_semaphore()
+    for k in FAR_FIRST:
+        pl.semaphore_signal(barrier, inc=1, device_id={"expert": peer(k)}, device_id_type=MESH)
+    pl.semaphore_signal(barrier, inc=1, device_id=partner, device_id_type=MESH)
+    for copy in small:
+        copy.wait()
 
     ids = ids_ref[...]
     named = one_hot(iota((experts, tok), 0) == ids)
@@ -124,7 +131,7 @@
         send_left[a] = left.astype(BF)
 
     def send_all(a):
-        for k in range(1, experts):
+        for k in FAR_FIRST:
             for copy in dispatch(a, k):
                 copy.start()
         own = pl.ds(pl.multiple_of(me * 16, 16), 16)
@@ -134,7 +141,7 @@
     def forward_all(a):
         for copy in forward(a, 0):
             copy.start()
-        for k in range(1, experts):
+        for k in reversed(FAR_FIRST):
             for copy in dispatch(a, k):
                 copy.wait_recv()
             for copy in forward(a, k):
@@ -145,20 +152,21 @@
             for copy in forward(a, k):
                 copy.wait_recv()
 
-    def spread_left(a):
+    def spread_left(a, h):
         r, c = iota((experts * extra, main), 0), iota((experts * extra, main), 1)
         for q in range(4):
             pick = one_hot(c == (r // extra) * 16 + q * extra + r % extra)
-            for h in range(2):
-                x_all[a, main:, pl.ds(h * half + q * quarter, quarter)] = dot(pick, left_all[a, h]).astype(BF)
+            at = pl.ds(pl.multiple_of(h * half + q * quarter, 128), quarter)
+            x_all[a, main:, at] = dot(pick, left_all[a, h]).astype(BF)
 
     loads[0].wait()
+    loads[1].wait()
+    for copy in weights:
+        copy.start()
     arrange(0)
     pl.semaphore_wait(barrier, peers + 1)
     send_all(0)
-    loads[1].wait()
     arrange(1)
-    send_all(1)
 
     place = one_hot(iota((tok, tok), 0) == layout_ref[...])
     pick_main[...] = dot_t(place, to_main).astype(BF)
@@ -166,15 +174,23 @@
         pick_left[q] = dot_t(place, to_left[q]).astype(BF)
     gate_row[...] = jnp.sum(jnp.where(iota((tok, tok), 0) == layout_ref[...], gates, 0.0), axis=1, keepdims=True)
 
+    for k in FAR_FIRST:
+        for copy in dispatch(0, k):
+            copy.wait_send()
+    send_all(1)
+
     forward_all(0)
     for copy in weights:
         copy.wait()
+    here, there = pl.ds(mine, half), pl.ds(other, half)
+    spread_left(0, core)
+    pre_gate[...] = dot(x_all[0, :, here], wg[here, :])
+    pre_up[...] = dot(x_all[0, :, here], wu[here, :])
     forward_wait(0)
-    spread_left(0)
-    pre_gate[...] = dot(x_all[0], wg[...])
-    pre_up[...] = dot(x_all[0], wu[...])
+    spread_left(0, 1 - core)
+    pre_gate[...] += dot(x_all[0, :, there], wg[there, :])
+    pre_up[...] += dot(x_all[0, :, there], wu[there, :])
     hidden[...] = (pre_gate[...] * jax.nn.sigmoid(pre_gate[...]) * pre_up[...]).astype(BF)
-    forward_all(1)
 
     def exchange(a):
         return pltpu.make_async_remote_copy(
@@ -214,7 +230,7 @@
             pick = one_hot(r == (c // extra) * 16 + q * extra + c % extra)
             packed = packed + dot(pick, total[main:])
         back_left[a] = packed.astype(BF)
-        for k in range(1, experts):
+        for k in FAR_FIRST:
             for copy in give_back(a, k):
                 copy.start()
         own = pl.ds(pl.multiple_of(me * 16, 16), 16)
@@ -224,11 +240,14 @@
     out_part(other, part_away)
     exchange(0).start()
     out_part(mine, part_home)
+    return_all(0)
+
+    forward_all(1)
+    spread_left(1, core)
+    grad_hidden = dot_t(x_all[1, :, here], wd[:, here])
     forward_wait(1)
-    spread_left(1)
-    return_all(0)
-
-    grad_hidden = dot_t(x_all[1], wd[...])
+    spread_left(1, 1 - core)
+    grad_hidden += dot_t(x_all[1, :, there], wd[:, there])
     gate_v, up_v = pre_gate[...], pre_up[...]
     sigma = jax.nn.sigmoid(gate_v)
     grad_gate[...] = (grad_hidden * up_v * sigma * (1.0 + gate_v * (1.0 - sigma))).astype(BF)
@@ -269,8 +288,9 @@
 
     for a, ref in ((0, out_ref), (1, grad_ref)):
         for k in range(1, experts):
-            for copy in dispatch(a, k):
-                copy.wait_send()
+            if a == 1:
+                for copy in dispatch(a, k):
+                    copy.wait_send()
             for copy in give_back(a, k):
                 copy.wait_send()
         for k in range(experts):
@@ -278,6 +298,14 @@
                 copy.wait_send()
         exchange(a).wait_send()
         finish_copy(a, ref).wait()
+
+
+def flush(a_ref, b_ref, a_hbm, b_hbm, sem):
+    copies = [pltpu.make_async_copy(a_ref, a_hbm, sem.at[0]), pltpu.make_async_copy(b_ref, b_hbm, sem.at[1])]
+    for copy in copies:
+        copy.start()
+    for copy in copies:
+        copy.wait()
 
 
 def shards(tokens, grads_out, expert_ids, gate_weights, layout_map, gate_w, up_w, down_w):
@@ -291,12 +319,15 @@
     vmem, dma = pltpu.VMEM, pltpu.SemaphoreType.DMA
     in_vmem, anywhere = pl.BlockSpec(memory_space=pltpu.VMEM), pl.BlockSpec(memory_space=pl.ANY)
     out = jax.ShapeDtypeStruct((tok // 2, width), BF)
-    return pl.pallas_call(
+    placed = pl.pallas_call(
         functools.partial(kernel, experts, cap),
-        out_shape=(out, out),
-        in_specs=[in_vmem] * 3 + [anywhere] * 5,
+        out_shape=(vmem(out.shape, BF), vmem(out.shape, BF)),
+        in_specs=[anywhere] * 8,
         out_specs=(in_vmem, in_vmem),
         scratch_shapes=[
+            vmem((1, tok), jnp.int32),
+            vmem((1, tok), F32),
+            vmem((1, tok), jnp.int32),
             vmem((2, tok, half), BF),
             vmem((2, main, half), BF),
             vmem((2, main, quarter), BF),
@@ -321,7 +352,7 @@
             vmem((4, tok, main), BF),
             vmem((tok, 1), F32),
             vmem((2, tok // 2, half), BF),
-            dma((2,)),
+            dma((5,)),
             dma((3,)),
             dma((2, experts, 2)),
             dma((2, experts, 2)),
@@ -345,6 +376,13 @@
         up_w[0],
         down_w[0],
     )
+    return pl.pallas_call(
+        flush,
+        out_shape=(out, out),
+        in_specs=[in_vmem, in_vmem],
+        out_specs=(anywhere, anywhere),
+        scratch_shapes=[dma((2,))],
+    )(*(pltpu.with_memory_space_constraint(value, pltpu.VMEM) for value in placed))
 
 
 def solution(mesh):

time: 62.8 us -> 51.8 us (0.82)
  Pallas kernels: 58.1 us -> 51 us
  local copies, waits for them, and re-layouts: 3.74 us -> 0 us
    pallas_call x1 -> x2, Pallas kernels: 58.1 us -> 51 us  [the longest x1 50 us: shards(): pl.pallas_call(functools.partial(kernel, experts, cap), out_shape=(vmem(o...]
    unnamed x2 -> x0, local copies, waits for them, and re-layouts: 3.74 us -> none
where the time goes in v2:
time: 51.8 us; the launch traced here: 51.6 us
  Pallas kernels  51 us (98%)
  between operations  0.64 us (1%)
    pallas_call x1, Pallas kernels, shards(): pl.pallas_call(functools.partial(kernel, experts, cap), out_shape=(vmem(o...  50 us

profile of v2, /device:TPU:1, one launch (start us, length us, event | category | flops | bytes accessed | tf_op | source)
XLA Modules:
  0.0 51.6 jit_solution(17541556974791120019)
XLA Ops:
  0.6 50.0 %shard_map.95 = (bf16[64,4096]{1,0:T(8,128)(2,1)S(1)}, bf16[64,4096]{1,0:T(8,128)(2,1)S(1)}) custom-call(s32[1,128]{1,0:T(1,128)} %bitcast.9, f32[1,128]{1,0:T(1,128)} %bitcast.10, s32[1,128]{1,0:T(1,128)} %bitcast.11, bf16[128,4096]{1,0:T(8,128)(2,1)} %tokens_ref.1, bf16[128,4096]{1,0:T(8,128)(2,1)} %grads_ref.1, bf16[4096,384]{1,0:T(8,128)(2,1)} %bitcast.6, ...), custom_call_target="tpu_custom_call" | custom-call | tf_op jit(solution)/shard_map/pallas_call | solution.py:322
  50.6 1.0 %shard_map.96 = (bf16[64,4096]{1,0:T(8,128)(2,1)}, bf16[64,4096]{1,0:T(8,128)(2,1)}) custom-call(bf16[64,4096]{1,0:T(8,128)(2,1)S(1)} %get-tuple-element.4.a_ref, bf16[64,4096]{1,0:T(8,128)(2,1)S(1)} %get-tuple-element.5.b_ref), custom_call_target="tpu_custom_call" | custom-call | tf_op jit(solution)/shard_map/pallas_call | solution.py:379

commit v3 on v2

--- a/solution.py
+++ b/solution.py
@@ -34,8 +34,8 @@
     out_ref, grad_ref,
     ids_ref, gates_ref, layout_ref, rows, send_main, send_left, x_all, left_all, wg, wu, wd,
     pre_gate, pre_up, hidden, grad_gate, grad_up, part_away, part_home, part_recv,
-    back_main, back_left, home_main, home_left, pick_main, pick_left, gate_row, away_out,
-    in_sem, w_sem, disp_s, disp_r, fwd_s, fwd_r, part_s, part_r, ret_s, ret_r, end_s, end_r,
+    back_main, back_left, home_main, home_left, pick_main, pick_left, gate_row, away_out, keep_out,
+    in_sem, w_sem, disp_s, disp_r, fwd_s, fwd_r, part_s, part_r, ret_s, ret_r, end_s, end_r, end_l,
 ):
     me, core = lax.axis_index("expert"), lax.axis_index("tensor")
     tok, width = tokens_ref.shape
@@ -174,9 +174,8 @@
         pick_left[q] = dot_t(place, to_left[q]).astype(BF)
     gate_row[...] = jnp.sum(jnp.where(iota((tok, tok), 0) == layout_ref[...], gates, 0.0), axis=1, keepdims=True)
 
-    for k in FAR_FIRST:
-        for copy in dispatch(0, k):
-            copy.wait_send()
+    for copy in dispatch(0, FAR_FIRST[0]):
+        copy.wait_send()
     send_all(1)
 
     forward_all(0)
@@ -192,55 +191,60 @@
     pre_up[...] += dot(x_all[0, :, there], wu[there, :])
     hidden[...] = (pre_gate[...] * jax.nn.sigmoid(pre_gate[...]) * pre_up[...]).astype(BF)
 
-    def exchange(a):
+    def exchange(a, q):
+        cols = pl.ds(q * quarter, quarter)
         return pltpu.make_async_remote_copy(
-            part_away.at[a], part_recv.at[a], part_s.at[a], part_r.at[a], device_id=partner, device_id_type=MESH)
-
-    def out_part(start, ref):
-        for q in range(4):
-            cols = pl.ds(q * quarter, quarter)
-            ref[0, :, cols] = dot(hidden[...], wd[:, pl.ds(pl.multiple_of(start + q * quarter, 128), quarter)]).astype(BF)
-
-    def grad_part(start, ref):
-        for q in range(4):
-            cols = pl.ds(q * quarter, quarter)
-            at = pl.ds(pl.multiple_of(start + q * quarter, 128), quarter)
-            ref[1, :, cols] = (dot_t(grad_gate[...], wg[at, :]) + dot_t(grad_up[...], wu[at, :])).astype(BF)
+            part_away.at[a, :, cols], part_recv.at[a, :, cols], part_s.at[a, q], part_r.at[a, q],
+            device_id=partner, device_id_type=MESH)
+
+    def out_part(start, q):
+        return dot(hidden[...], wd[:, pl.ds(pl.multiple_of(start + q * quarter, 128), quarter)]).astype(BF)
+
+    def grad_part(start, q):
+        at = pl.ds(pl.multiple_of(start + q * quarter, 128), quarter)
+        return (dot_t(grad_gate[...], wg[at, :]) + dot_t(grad_up[...], wu[at, :])).astype(BF)
 
     def give_back(a, k):
         g = peer(k)
         here, there = pl.ds(pl.multiple_of(g * 16, 16), 16), pl.ds(pl.multiple_of(me * 16, 16), 16)
-        return (
-            pltpu.make_async_remote_copy(
-                back_main.at[a, here], home_main.at[a, there],
-                ret_s.at[a, k, 0], ret_r.at[a, k, 0], device_id={"expert": g}, device_id_type=MESH),
+        return [
+            pltpu.make_async_remote_copy(
+                back_main.at[a, here, pl.ds(q * quarter, quarter)], home_main.at[a, there, pl.ds(q * quarter, quarter)],
+                ret_s.at[a, k, q], ret_r.at[a, k, q], device_id={"expert": g}, device_id_type=MESH)
+            for q in range(4)
+        ] + [
             pltpu.make_async_remote_copy(
                 back_left.at[a, here], home_left.at[a, there],
-                ret_s.at[a, k, 1], ret_r.at[a, k, 1], device_id={"expert": g}, device_id_type=MESH),
-        )
-
-    def return_all(a):
-        exchange(a).wait_recv()
+                ret_s.at[a, k, 4], ret_r.at[a, k, 4], device_id={"expert": g}, device_id_type=MESH)
+        ]
+
+    def return_all(a, part):
         r, c = iota((main, experts * extra), 0), iota((main, experts * extra), 1)
         packed = jnp.zeros((main, quarter), F32)
-        for q in range(4):
-            cols = pl.ds(q * quarter, quarter)
-            total = (part_home[a, :, cols].astype(F32) + part_recv[a, :, cols].astype(F32)).astype(BF)
-            back_main[a, :, cols] = total[:main]
-            pick = one_hot(r == (c // extra) * 16 + q * extra + c % extra)
-            packed = packed + dot(pick, total[main:])
+        for step in range(6):
+            if step < 4:
+                part_away[a, :, pl.ds(step * quarter, quarter)] = part(other, step)
+                exchange(a, step).start()
+            if 1 <= step < 5:
+                part_home[a, :, pl.ds((step - 1) * quarter, quarter)] = part(mine, step - 1)
+            if step >= 2:
+                q = step - 2
+                cols = pl.ds(q * quarter, quarter)
+                exchange(a, q).wait_recv()
+                total = (part_home[a, :, cols].astype(F32) + part_recv[a, :, cols].astype(F32)).astype(BF)
+                back_main[a, :, cols] = total[:main]
+                pick = one_hot(r == (c // extra) * 16 + q * extra + c % extra)
+                packed = packed + dot(pick, total[main:])
+                for k in FAR_FIRST:
+                    give_back(a, k)[q].start()
         back_left[a] = packed.astype(BF)
         for k in FAR_FIRST:
-            for copy in give_back(a, k):
-                copy.start()
+            give_back(a, k)[4].start()
         own = pl.ds(pl.multiple_of(me * 16, 16), 16)
         home_main[a, own] = back_main[a, own]
         home_left[a, own] = back_left[a, own]
 
-    out_part(other, part_away)
-    exchange(0).start()
-    out_part(mine, part_home)
-    return_all(0)
+    return_all(0, out_part)
 
     forward_all(1)
     spread_left(1, core)
@@ -252,15 +256,15 @@
     sigma = jax.nn.sigmoid(gate_v)
     grad_gate[...] = (grad_hidden * up_v * sigma * (1.0 + gate_v * (1.0 - sigma))).astype(BF)
     grad_up[...] = (grad_hidden * gate_v * sigma).astype(BF)
-    grad_part(other, part_away)
-    exchange(1).start()
-    grad_part(mine, part_home)
-    return_all(1)
+    return_all(1, grad_part)
 
     def finish_copy(a, ref):
         return pltpu.make_async_remote_copy(
             away_out.at[a], ref.at[:, pl.ds(mine, half)], end_s.at[a], end_r.at[a],
             device_id=partner, device_id_type=MESH)
+
+    def keep_copy(a, ref):
+        return pltpu.make_async_copy(keep_out.at[a], ref.at[:, pl.ds(mine, half)], end_l.at[a])
 
     keep = pl.ds(pl.multiple_of(core * half_rows, half_rows), half_rows)
     give = pl.ds(pl.multiple_of((1 - core) * half_rows, half_rows), half_rows)
@@ -281,14 +285,15 @@
             away_out[a, :, pl.ds(q * quarter, quarter)] = placed(give, q)
         finish_copy(a, ref).start()
         for q in range(4):
-            ref[:, pl.ds(pl.multiple_of(mine + q * quarter, 128), quarter)] = placed(keep, q)
+            keep_out[a, :, pl.ds(q * quarter, quarter)] = placed(keep, q)
+        keep_copy(a, ref).start()
 
     finish(0, out_ref)
     finish(1, grad_ref)
 
     for a, ref in ((0, out_ref), (1, grad_ref)):
         for k in range(1, experts):
-            if a == 1:
+            if a == 1 or k != FAR_FIRST[0]:
                 for copy in dispatch(a, k):
                     copy.wait_send()
             for copy in give_back(a, k):
@@ -296,7 +301,9 @@
         for k in range(experts):
             for copy in forward(a, k):
                 copy.wait_send()
-        exchange(a).wait_send()
+        for q in range(4):
+            exchange(a, q).wait_send()
+        keep_copy(a, ref).wait()
         finish_copy(a, ref).wait()
 
 
@@ -317,13 +324,13 @@
     quarter = half // 4
     slots, main = experts * cap, experts * 16
     vmem, dma = pltpu.VMEM, pltpu.SemaphoreType.DMA
-    in_vmem, anywhere = pl.BlockSpec(memory_space=pltpu.VMEM), pl.BlockSpec(memory_space=pl.ANY)
+    anywhere = pl.BlockSpec(memory_space=pl.ANY)
     out = jax.ShapeDtypeStruct((tok // 2, width), BF)
     placed = pl.pallas_call(
         functools.partial(kernel, experts, cap),
         out_shape=(vmem(out.shape, BF), vmem(out.shape, BF)),
         in_specs=[anywhere] * 8,
-        out_specs=(in_vmem, in_vmem),
+        out_specs=(anywhere, anywhere),
         scratch_shapes=[
             vmem((1, tok), jnp.int32),
             vmem((1, tok), F32),
@@ -352,16 +359,18 @@
             vmem((4, tok, main), BF),
             vmem((tok, 1), F32),
             vmem((2, tok // 2, half), BF),
+            vmem((2, tok // 2, half), BF),
             dma((5,)),
             dma((3,)),
             dma((2, experts, 2)),
             dma((2, experts, 2)),
             dma((2, experts, 2)),
             dma((2, experts, 2)),
+            dma((2, 4)),
+            dma((2, 4)),
+            dma((2, experts, 5)),
+            dma((2, experts, 5)),
             dma((2,)),
-            dma((2,)),
-            dma((2, experts, 2)),
-            dma((2, experts, 2)),
             dma((2,)),
             dma((2,)),
         ],
@@ -379,7 +388,7 @@
     return pl.pallas_call(
         flush,
         out_shape=(out, out),
-        in_specs=[in_vmem, in_vmem],
+        in_specs=[anywhere, anywhere],
         out_specs=(anywhere, anywhere),
         scratch_shapes=[dma((2,))],
     )(*(pltpu.with_memory_space_constraint(value, pltpu.VMEM) for value in placed))

time: 51.8 us -> 53.2 us (1.027)
  Pallas kernels: 51 us -> 52.4 us
    pallas_call x1, Pallas kernels: 50 us -> 51.4 us  [shards(): pl.pallas_call(functools.partial(kernel, experts, cap), out_shape=(vmem(o...]
where the time goes in v3:
time: 53.2 us; the launch traced here: 53 us
  Pallas kernels  52.4 us (98%)
  between operations  0.64 us (1%)
    pallas_call x1, Pallas kernels, shards(): pl.pallas_call(functools.partial(kernel, experts, cap), out_shape=(vmem(o...  51.4 us

profile of v3, /device:TPU:1, one launch (start us, length us, event | category | flops | bytes accessed | tf_op | source)
XLA Modules:
  0.0 53.0 jit_solution(11508159629005604722)
XLA Ops:
  0.6 51.4 %shard_map.95 = (bf16[64,4096]{1,0:T(8,128)(2,1)S(1)}, bf16[64,4096]{1,0:T(8,128)(2,1)S(1)}) custom-call(s32[1,128]{1,0:T(1,128)} %bitcast.9, f32[1,128]{1,0:T(1,128)} %bitcast.10, s32[1,128]{1,0:T(1,128)} %bitcast.11, bf16[128,4096]{1,0:T(8,128)(2,1)} %tokens_ref.1, bf16[128,4096]{1,0:T(8,128)(2,1)} %grads_ref.1, bf16[4096,384]{1,0:T(8,128)(2,1)} %bitcast.6, ...), custom_call_target="tpu_custom_call" | custom-call | tf_op jit(solution)/shard_map/pallas_call | solution.py:329
  52.0 1.0 %shard_map.96 = (bf16[64,4096]{1,0:T(8,128)(2,1)}, bf16[64,4096]{1,0:T(8,128)(2,1)}) custom-call(bf16[64,4096]{1,0:T(8,128)(2,1)S(1)} %get-tuple-element.4.a_ref, bf16[64,4096]{1,0:T(8,128)(2,1)S(1)} %get-tuple-element.5.b_ref), custom_call_target="tpu_custom_call" | custom-call | tf_op jit(solution)/shard_map/pallas_call | solution.py:388
